TPU v7x, 32 devices: a whole 2x2x4 slice. The times are simulated.
32 devices in a mesh: scene: 2 (over x), seq: 16 (over z, y, core).
Axes of the slice: x: 2, y: 2, z: 4, core: 2. Of those that a mesh axis runs over, the one named last changes fastest.
Arguments:
- tokens: bfloat16 [2, 4096, 1024], P('scene', 'seq'), may hold values from -6 to 6
- surface_mask: int32 [2, 4096], P('scene', 'seq'), may hold values 0 or 1
- out_grad: bfloat16 [2, 4096, 1024], P('scene', 'seq'), may hold values from -6 to 6
- w_query: bfloat16 [1024, 1024], replicated, may hold values from -0.1875 to 0.1875
- w_key: bfloat16 [1024, 1024], replicated, may hold values from -0.1875 to 0.1875
- w_value: bfloat16 [1024, 1024], replicated, may hold values from -0.1875 to 0.1875
- w_out: bfloat16 [1024, 1024], replicated, may hold values from -6 to 6
- w_up: bfloat16 [1024, 4096], replicated, may hold values from -0.1875 to 0.1875
- w_down: bfloat16 [4096, 1024], replicated, may hold values from -0.09375 to 0.09375
- b_query: float32 [1024], replicated, may hold values from -3 to 3
- b_value: float32 [1024], replicated, may hold values from -3 to 3
- b_out: float32 [1024], replicated, may hold values from -3 to 3
- b_up: float32 [4096], replicated, may hold values from -3 to 3
- b_down: float32 [1024], replicated, may hold values from -3 to 3
- gain_one: float32 [1024], replicated, may hold values from 0.1 to 1.9
- shift_one: float32 [1024], replicated, may hold values from -3 to 3
- gain_two: float32 [1024], replicated, may hold values from 0.1 to 1.9
- shift_two: float32 [1024], replicated, may hold values from -3 to 3
Outputs:
- block_out: bfloat16 [2, 4096, 1024], P('scene', 'seq')
- tokens_grad: bfloat16 [2, 4096, 1024], P('scene', 'seq')
- query_grad: float32 [1024, 1024], P(('scene', 'seq'))
- key_grad: float32 [1024, 1024], P(('scene', 'seq'))
- value_grad: float32 [1024, 1024], P(('scene', 'seq'))
- out_proj_grad: float32 [1024, 1024], P(('scene', 'seq'))
- up_grad: float32 [1024, 4096], P(('scene', 'seq'))
- down_grad: float32 [4096, 1024], P(('scene', 'seq'))
- query_bias_grad: float32 [1024], P(('scene', 'seq'))
- value_bias_grad: float32 [1024], P(('scene', 'seq'))
- out_bias_grad: float32 [1024], P(('scene', 'seq'))
- up_bias_grad: float32 [4096], P(('scene', 'seq'))
- down_bias_grad: float32 [1024], P(('scene', 'seq'))
- gain_one_grad: float32 [1024], P(('scene', 'seq'))
- shift_one_grad: float32 [1024], P(('scene', 'seq'))
- gain_two_grad: float32 [1024], P(('scene', 'seq'))
- shift_two_grad: float32 [1024], P(('scene', 'seq'))
All inputs are finite; a program needn't handle non-finite values. No bound on the sum of `surface_mask` on one device may be relied on, other than what follows from the above.
Results may differ from a plain program's by a relative error of at most 0.014.
Values may be sent and summed in bfloat16 or wider, within the bound.
A program may use at most 320 MiB of HBM per device.

v0:
```python
import jax
import jax.numpy as jnp
from jax import lax
from jax.sharding import PartitionSpec as P

HEADS = 16
HEAD_DIM = 64
norm_eps = 1e-05
score_scale = 0.125
gelu_coef = 0.7978845608028654


def norm_rows(values, gain, shift):
    row_mean = jnp.mean(values, axis=-1, keepdims=True)
    centred = values - row_mean
    row_var = jnp.mean(centred * centred, axis=-1, keepdims=True)
    return centred * lax.rsqrt(row_var + norm_eps) * gain + shift


def gelu_tanh(values):
    return (
        0.5 * values * (1.0 + jnp.tanh(gelu_coef * (values + 0.044715 * values * values * values)))
    )


def matmul(left, right):
    return jnp.dot(left, right, preferred_element_type=jnp.float32)


def matmul_tn(left, right):
    return lax.dot_general(
        left, right, (((0,), (0,)), ((), ())), preferred_element_type=jnp.float32
    )


def matmul_nt(left, right):
    return lax.dot_general(
        left, right, (((1,), (1,)), ((), ())), preferred_element_type=jnp.float32
    )


def take_pair(array_in, pair_index):
    pair_width = 2 * HEAD_DIM
    sliced = lax.dynamic_slice_in_dim(array_in, pair_index * pair_width, pair_width, 2)
    return sliced.reshape(sliced.shape[:2] + (2, HEAD_DIM))


def take_stats(array_in, pair_index):
    return lax.dynamic_slice_in_dim(array_in, pair_index * 2, 2, 1)


def join_pairs(stacked):
    moved = jnp.moveaxis(stacked, 0, 2)
    return moved.reshape(moved.shape[:2] + (moved.shape[2] * moved.shape[3],))


def join_stats(stacked):
    moved = jnp.moveaxis(stacked, 0, 1)
    return moved.reshape((moved.shape[0], moved.shape[1] * moved.shape[2], moved.shape[3]))


def merge_heads(pair_part):
    return pair_part.reshape(pair_part.shape[:2] + (2 * HEAD_DIM,))


def attend(q_scene, k_gathered, v_gathered):

    def attend_pair_step(unused, pair_index):
        q_pair = take_pair(q_scene, pair_index)
        k_pair = take_pair(k_gathered, pair_index)
        v_pair = take_pair(v_gathered, pair_index)
        scores = (
            jnp.einsum("sqhe,skhe->shqk", q_pair, k_pair, preferred_element_type=jnp.float32)
            * score_scale
        )
        row_max = jnp.max(scores, axis=-1, keepdims=True)
        shifted = jnp.exp(scores - row_max)
        row_sum = jnp.sum(shifted, axis=-1, keepdims=True)
        prob_low = (shifted / row_sum).astype(jnp.bfloat16)
        pair_out = jnp.einsum(
            "shqk,skhe->sqhe", prob_low, v_pair, preferred_element_type=jnp.float32
        )
        pair_lse = (row_max + jnp.log(row_sum))[..., 0]
        return (unused, (merge_heads(pair_out), pair_lse))

    pair_count = HEADS // 2
    _, (pair_outs, pair_lses) = lax.scan(
        attend_pair_step, jnp.zeros((), jnp.float32), jnp.arange(pair_count, dtype=jnp.int32)
    )
    return (join_pairs(pair_outs), join_stats(pair_lses))


def query_side(q_scene, k_gathered, v_gathered, row_lse, att_grad):

    def query_pair_step(unused, pair_index):
        q_pair = take_pair(q_scene, pair_index)
        k_pair = take_pair(k_gathered, pair_index)
        v_pair = take_pair(v_gathered, pair_index)
        d_pair = take_pair(att_grad, pair_index)
        l_pair = take_stats(row_lse, pair_index)
        scores = (
            jnp.einsum("sqhe,skhe->shqk", q_pair, k_pair, preferred_element_type=jnp.float32)
            * score_scale
        )
        attn_prob = jnp.exp(scores - l_pair[..., None])
        dprob = jnp.einsum("sqhe,skhe->shqk", d_pair, v_pair, preferred_element_type=jnp.float32)
        row_delta = jnp.sum(attn_prob * dprob, axis=-1)
        dscore = (attn_prob * (dprob - row_delta[..., None])).astype(jnp.bfloat16)
        q_part = (
            jnp.einsum("shqk,skhe->sqhe", dscore, k_pair, preferred_element_type=jnp.float32)
            * score_scale
        )
        results = (merge_heads(q_part), row_delta)
        prob_low = attn_prob.astype(jnp.bfloat16)
        k_part = (
            jnp.einsum("shqk,sqhe->skhe", dscore, q_pair, preferred_element_type=jnp.float32)
            * score_scale
        )
        v_part = jnp.einsum("shqk,sqhe->skhe", prob_low, d_pair, preferred_element_type=jnp.float32)
        results = results + (merge_heads(k_part), merge_heads(v_part))
        return (unused, results)

    pair_count = HEADS // 2
    _, results = lax.scan(
        query_pair_step, jnp.zeros((), jnp.float32), jnp.arange(pair_count, dtype=jnp.int32)
    )
    return results


def on_device(
    tokens,
    surface_mask,
    out_grad,
    w_query,
    w_key,
    w_value,
    w_out,
    w_up,
    w_down,
    b_query,
    b_value,
    b_out,
    b_up,
    b_down,
    gain_one,
    shift_one,
    gain_two,
    shift_two,
):
    scenes, local_len, model_width = tokens.shape
    row_count = scenes * local_len
    flat_rows = tokens.astype(jnp.float32).reshape(row_count, model_width)
    normed, norm_one_pull = jax.vjp(norm_rows, flat_rows, gain_one, shift_one)
    normed_low = normed.astype(jnp.bfloat16)
    q_low = (matmul(normed_low, w_query) + b_query).astype(jnp.bfloat16)
    k_low = matmul(normed_low, w_key).astype(jnp.bfloat16)
    v_low = (matmul(normed_low, w_value) + b_value).astype(jnp.bfloat16)
    q_scene = q_low.reshape(scenes, local_len, model_width)
    k_scene = k_low.reshape(scenes, local_len, model_width)
    v_scene = v_low.reshape(scenes, local_len, model_width)
    k_gathered, v_gathered = (
        lax.all_gather(k_scene, "seq", axis=1, tiled=True),
        lax.all_gather(v_scene, "seq", axis=1, tiled=True),
    )
    attended, row_lse = attend(q_scene, k_gathered, v_gathered)
    att_low = attended.reshape(row_count, model_width).astype(jnp.bfloat16)
    residual = flat_rows + matmul(att_low, w_out) + b_out
    normed_two, norm_two_pull = jax.vjp(norm_rows, residual, gain_two, shift_two)
    normed_two_low = normed_two.astype(jnp.bfloat16)
    hidden = matmul(normed_two_low, w_up) + b_up
    activated, gelu_pull = jax.vjp(gelu_tanh, hidden)
    act_low = activated.astype(jnp.bfloat16)
    block_rows = residual + matmul(act_low, w_down) + b_down
    block_out = block_rows.reshape(scenes, local_len, model_width).astype(jnp.bfloat16)
    masked_f = out_grad.astype(jnp.float32) * surface_mask.astype(jnp.float32)[..., None]
    masked_rows = masked_f.reshape(row_count, model_width)
    masked_low = masked_rows.astype(jnp.bfloat16)
    grad_down = matmul_tn(act_low, masked_low)
    grad_bdown = jnp.sum(masked_rows, axis=0)
    act_grad = matmul_nt(masked_low, w_down)
    hidden_low = gelu_pull(act_grad)[0].astype(jnp.bfloat16)
    grad_up = matmul_tn(normed_two_low, hidden_low)
    grad_bup = jnp.sum(hidden_low.astype(jnp.float32), axis=0)
    norm_two_in = matmul_nt(hidden_low, w_up)
    resid_part, grad_gain_two, grad_shift_two = norm_two_pull(norm_two_in)
    resid_grad = masked_rows + resid_part
    resid_low = resid_grad.astype(jnp.bfloat16)
    grad_out = matmul_tn(att_low, resid_low)
    grad_bout = jnp.sum(resid_low.astype(jnp.float32), axis=0)
    att_grad = (
        matmul_nt(resid_low, w_out).astype(jnp.bfloat16).reshape(scenes, local_len, model_width)
    )
    q_parts, delta_parts, k_parts, v_parts = query_side(
        q_scene, k_gathered, v_gathered, row_lse, att_grad
    )
    k_summed, v_summed = (
        lax.psum_scatter(
            k_parts.astype(jnp.bfloat16), "seq", scatter_dimension=2, tiled=True
        ).astype(jnp.float32),
        lax.psum_scatter(
            v_parts.astype(jnp.bfloat16), "seq", scatter_dimension=2, tiled=True
        ).astype(jnp.float32),
    )
    k_grad = join_pairs(k_summed)
    v_grad = join_pairs(v_summed)
    q_grad = join_pairs(q_parts)
    q_grad_low = q_grad.reshape(row_count, model_width).astype(jnp.bfloat16)
    k_grad_low = k_grad.reshape(row_count, model_width).astype(jnp.bfloat16)
    v_grad_low = v_grad.reshape(row_count, model_width).astype(jnp.bfloat16)
    grad_query = matmul_tn(normed_low, q_grad_low)
    grad_key = matmul_tn(normed_low, k_grad_low)
    grad_value = matmul_tn(normed_low, v_grad_low)
    grad_bquery = jnp.sum(q_grad_low.astype(jnp.float32), axis=0)
    grad_bvalue = jnp.sum(v_grad_low.astype(jnp.float32), axis=0)
    norm_one_in = (
        matmul_nt(q_grad_low, w_query)
        + matmul_nt(k_grad_low, w_key)
        + matmul_nt(v_grad_low, w_value)
    )
    token_part, grad_gain_one, grad_shift_one = norm_one_pull(norm_one_in)
    tokens_grad = (
        (resid_grad + token_part).reshape(scenes, local_len, model_width).astype(jnp.bfloat16)
    )
    (
        sum_query,
        sum_key,
        sum_value,
        sum_out,
        sum_bquery,
        sum_bvalue,
        sum_bout,
        sum_gain_one,
        sum_shift_one,
        sum_up,
        sum_down,
        sum_bup,
        sum_bdown,
        sum_gain_two,
        sum_shift_two,
    ) = (
        lax.psum_scatter(grad_query, ("scene", "seq"), scatter_dimension=0, tiled=True),
        lax.psum_scatter(grad_key, ("scene", "seq"), scatter_dimension=0, tiled=True),
        lax.psum_scatter(grad_value, ("scene", "seq"), scatter_dimension=0, tiled=True),
        lax.psum_scatter(grad_out, ("scene", "seq"), scatter_dimension=0, tiled=True),
        lax.psum_scatter(grad_bquery, ("scene", "seq"), scatter_dimension=0, tiled=True),
        lax.psum_scatter(grad_bvalue, ("scene", "seq"), scatter_dimension=0, tiled=True),
        lax.psum_scatter(grad_bout, ("scene", "seq"), scatter_dimension=0, tiled=True),
        lax.psum_scatter(grad_gain_one, ("scene", "seq"), scatter_dimension=0, tiled=True),
        lax.psum_scatter(grad_shift_one, ("scene", "seq"), scatter_dimension=0, tiled=True),
        lax.psum_scatter(grad_up, ("scene", "seq"), scatter_dimension=0, tiled=True),
        lax.psum_scatter(grad_down, ("scene", "seq"), scatter_dimension=0, tiled=True),
        lax.psum_scatter(grad_bup, ("scene", "seq"), scatter_dimension=0, tiled=True),
        lax.psum_scatter(grad_bdown, ("scene", "seq"), scatter_dimension=0, tiled=True),
        lax.psum_scatter(grad_gain_two, ("scene", "seq"), scatter_dimension=0, tiled=True),
        lax.psum_scatter(grad_shift_two, ("scene", "seq"), scatter_dimension=0, tiled=True),
    )
    return (
        block_out,
        tokens_grad,
        sum_query,
        sum_key,
        sum_value,
        sum_out,
        sum_up,
        sum_down,
        sum_bquery,
        sum_bvalue,
        sum_bout,
        sum_bup,
        sum_bdown,
        sum_gain_one,
        sum_shift_one,
        sum_gain_two,
        sum_shift_two,
    )


def solution(mesh):
    placed = (
        P("scene", "seq", None),
        P("scene", "seq"),
        P("scene", "seq", None),
        P(),
        P(),
        P(),
        P(),
        P(),
        P(),
        P(),
        P(),
        P(),
        P(),
        P(),
        P(),
        P(),
        P(),
        P(),
    )
    return jax.shard_map(
        on_device,
        mesh=mesh,
        in_specs=placed,
        out_specs=(
            P("scene", "seq", None),
            P("scene", "seq", None),
            P(("scene", "seq"), None),
            P(("scene", "seq"), None),
            P(("scene", "seq"), None),
            P(("scene", "seq"), None),
            P(("scene", "seq"), None),
            P(("scene", "seq"), None),
            P(("scene", "seq")),
            P(("scene", "seq")),
            P(("scene", "seq")),
            P(("scene", "seq")),
            P(("scene", "seq")),
            P(("scene", "seq")),
            P(("scene", "seq")),
            P(("scene", "seq")),
            P(("scene", "seq")),
        ),
        check_vma=False,
    )
```

profile of v0, /device:TPU:9, one launch (start us, length us, event | category | flops | bytes accessed | tf_op | source)
XLA Modules:
  0.0 1661.1 jit_solution(7076041561755759142)
XLA Ops:
  18.6 70.9 %all-gather.7.cloned.1.call-done = bf16[4096,1024]{1,0:T(8,128)(2,1)} async-done(((bf16[256,1024]{1,0:T(8,128)(2,1)}), bf16[4096,1024]{1,0:T(8,128)(2,1)}) %all-gather.7.cloned.1.call-update) | async-done | bytes 8388624 | tf_op jit(solution)/shard_map/all_gather | solution.py:162
  89.5 11.3 copy.44
  100.7 64.6 %all-gather.5.cloned.1.call-done = bf16[4096,1024]{1,0:T(8,128)(2,1)} async-done(((bf16[256,1024]{1,0:T(8,128)(2,1)}), bf16[4096,1024]{1,0:T(8,128)(2,1)}) %all-gather.5.cloned.1.call-update) | async-done | bytes 8388624 | tf_op jit(solution)/shard_map/all_gather | solution.py:163
  165.4 11.3 copy.42
  176.8 71.2 %while.26 = (s32[]{:T(128)}, bf16[8,1,256,128]{2,3,1,0:T(8,128)(2,1)S(1)}, f32[8,1,2,256]{3,2,1,0:T(2,128)S(1)}, s32[8]{0:T(128)S(1)}, bf16[1,4096,1024]{1,2,0:T...) while((s32[]{:T(128)}, ...), condition=%wide.region_5.6_spmd, body=%wide.region_2.5_spmd.sunk | while | flops 555744768 | bytes 31867072 | solution.py:87
  251.0 6.0 convolution_add_fusion
  257.1 6.5 convert_reduce_fusion
  271.5 234.4 %while.27 = (s32[]{:T(128)}, bf16[8,1,256,128]{2,3,1,0:T(8,128)(2,1)}, bf16[8,1,4096,128]{2,3,1,0:T(8,128)(2,1)}, bf16[8,1,4096,128]{2,3,1,0:T(8,128)(2,1)}, s32...) while((s32[]{:T(128)}, ...), condition=%wide.region_12.13_spmd, body=%wide.region_10.12_spmd.sunk | while | flops 1360068096 | bytes 123546016 | solution.py:124
  278.4 4.9 multiply_reduce_fusion.8
  284.1 7.9 multiply_convert_fusion.5
  307.7 4.9 multiply_reduce_fusion.8
  313.4 7.9 multiply_convert_fusion.5
  342.7 7.9 multiply_convert_fusion.5
  366.3 4.9 multiply_reduce_fusion.8
  372.0 7.9 multiply_convert_fusion.5
  395.6 4.9 multiply_reduce_fusion.8
  401.3 7.9 multiply_convert_fusion.5
  430.5 7.9 multiply_convert_fusion.5
  459.9 7.9 multiply_convert_fusion.5
  489.2 7.9 multiply_convert_fusion.5
  514.2 95.1 %reduce-scatter.11.cloned.1.call-done = bf16[8,1,256,128]{2,3,1,0:T(8,128)(2,1)} async-done(((bf16[8,1,4096,128]{2,3,1,0:T(8,128)(2,1)}), bf16[8,1,256,128]{2,3,1,0:T(8,128)(2,1)}) %reduce-scatter.11.cloned.1.call-update) | async-done | bytes 524304 | tf_op jit(solution)/shard_map/reduce_scatter | solution.py:200
  613.3 104.6 %reduce-scatter.9.cloned.1.call-done = bf16[8,1,256,128]{2,3,1,0:T(8,128)(2,1)} async-done(((bf16[8,1,4096,128]{2,3,1,0:T(8,128)(2,1)}), bf16[8,1,256,128]{2,3,1,0:T(8,128)(2,1)}) %reduce-scatter.9.cloned.1.call-update) | async-done | bytes 524304 | tf_op jit(solution)/shard_map/reduce_scatter | solution.py:197
  721.9 10.8 fusion.39
  733.4 10.2 fusion.44
  747.8 8.4 fusion.23
  759.8 40.0 %all-reduce.9 = (f32[1024]{0:T(1024)S(1)}, f32[1024]{0:T(1024)S(1)}, f32[1024]{0:T(1024)S(1)}, f32[4096]{0:T(1024)S(1)}, f32[1024]{0:T(1024)S(1)}, /*index=5*/f3...) all-reduce(f32[1024]{0:T(1024)S(1)} %bitcast.240, ...), channel_id=12, replica_groups=mesh['scene'=2,'seq'=16] {'scene','seq'}, use_global_device_ids=true, to_apply=%region_24.25.clone | all-reduce | flops 12288 | bytes 98304
  808.0 38.4 %reduce-scatter.19.cloned.1.call-done = f32[32,1024]{1,0:T(8,128)} async-done(((f32[1024,1024]{1,0:T(8,128)}), f32[32,1024]{1,0:T(8,128)}) %reduce-scatter.19.cloned.1.call-update) | async-done | bytes 131088 | tf_op jit(solution)/shard_map/reduce_scatter | solution.py:244
  846.4 139.8 %reduce-scatter.13.cloned.1.call-done = f32[32,1024]{1,0:T(8,128)} async-done(((f32[1024,1024]{1,0:T(8,128)}), f32[32,1024]{1,0:T(8,128)}) %reduce-scatter.13.cloned.1.call-update) | async-done | bytes 131088 | tf_op jit(solution)/shard_map/reduce_scatter | solution.py:241
  986.2 140.4 %reduce-scatter.17.cloned.1.call-done = f32[32,1024]{1,0:T(8,128)} async-done(((f32[1024,1024]{1,0:T(8,128)}), f32[32,1024]{1,0:T(8,128)}) %reduce-scatter.17.cloned.1.call-update) | async-done | bytes 131088 | tf_op jit(solution)/shard_map/reduce_scatter | solution.py:243
  1126.6 140.2 %reduce-scatter.15.cloned.1.call-done = f32[32,1024]{1,0:T(8,128)} async-done(((f32[1024,1024]{1,0:T(8,128)}), f32[32,1024]{1,0:T(8,128)}) %reduce-scatter.15.cloned.1.call-update) | async-done | bytes 131088 | tf_op jit(solution)/shard_map/reduce_scatter | solution.py:242
  1266.8 198.9 %reduce-scatter.23.cloned.1.call-done = f32[128,1024]{1,0:T(8,128)} async-done(((f32[4096,1024]{1,0:T(8,128)}), f32[128,1024]{1,0:T(8,128)}) %reduce-scatter.23.cloned.1.call-update) | async-done | bytes 524304 | tf_op jit(solution)/shard_map/reduce_scatter | solution.py:251
  1465.7 188.2 %reduce-scatter.21.cloned.1.call-done = f32[32,4096]{1,0:T(8,128)} async-done(((f32[1024,4096]{1,0:T(8,128)}), f32[32,4096]{1,0:T(8,128)}) %reduce-scatter.21.cloned.1.call-update) | async-done | bytes 524304 | tf_op jit(solution)/shard_map/reduce_scatter | solution.py:250
  (422 shorter events, 260.2 us)
Async XLA Ops:
  7.2 6.3 copy-start
  7.2 6.3 copy-start.4
  7.2 82.2 %all-gather.7.cloned.1.call-start = ((), (), s32[]{:S(2)}) async-start(), calls=%async_computation.17 | async-start | bytes 8912896 | tf_op jit(solution)/shard_map/all_gather | solution.py:162
  8.6 6.6 copy-start.30
  13.4 151.9 %all-gather.5.cloned.1.call-start = ((), (), s32[]{:S(2)}) async-start(), calls=%async_computation.16 | async-start | bytes 8912896 | tf_op jit(solution)/shard_map/all_gather | solution.py:163
  15.1 594.3 %reduce-scatter.11.cloned.1.call-start = ((), (), s32[]{:S(2)}) async-start(), calls=%async_computation.9 | async-start | bytes 8912896 | tf_op jit(solution)/shard_map/reduce_scatter | solution.py:200
  176.8 71.3 %copy-start.36 = (f32[1024]{0:T(1024)S(1)}, f32[1024]{0:T(1024)}, u32[]{:S(2)}) copy-start(f32[1024]{0:T(1024)} %param.33) | copy-start | bytes 12292
  248.0 9.0 copy-start.13
  248.1 9.0 slice-start.2
  250.7 16.1 copy-start.6
  251.0 12.6 slice-start
  257.0 6.6 copy-start.15
  257.1 6.5 slice-start.1
  271.5 6.9 copy-start.23
  300.7 6.9 copy-start.23
  330.0 6.9 copy-start.23
  359.3 6.9 copy-start.23
  388.6 6.9 copy-start.23
  417.9 6.9 copy-start.23
  447.2 6.9 copy-start.23
  476.5 6.9 copy-start.23
  505.9 212.0 %reduce-scatter.9.cloned.1.call-start = ((), (), s32[]{:S(2)}) async-start(), calls=%async_computation.8 | async-start | bytes 8912896 | tf_op jit(solution)/shard_map/reduce_scatter | solution.py:197
  506.5 340.0 %reduce-scatter.19.cloned.1.call-start = ((), (), s32[]{:S(2)}) async-start(), calls=%async_computation.13 | async-start | bytes 4325376 | tf_op jit(solution)/shard_map/reduce_scatter | solution.py:244
  509.9 476.4 %reduce-scatter.13.cloned.1.call-start = ((), (), s32[]{:S(2)}) async-start(), calls=%async_computation.10 | async-start | bytes 4325376 | tf_op jit(solution)/shard_map/reduce_scatter | solution.py:241
  514.2 612.4 %reduce-scatter.17.cloned.1.call-start = ((), (), s32[]{:S(2)}) async-start(), calls=%async_computation.12 | async-start | bytes 4325376 | tf_op jit(solution)/shard_map/reduce_scatter | solution.py:243
  613.2 653.6 %reduce-scatter.15.cloned.1.call-start = ((), (), s32[]{:S(2)}) async-start(), calls=%async_computation.11 | async-start | bytes 4325376 | tf_op jit(solution)/shard_map/reduce_scatter | solution.py:242
  721.8 743.9 %reduce-scatter.23.cloned.1.call-start = ((), (), s32[]{:S(2)}) async-start(), calls=%async_computation.15 | async-start | bytes 17301504 | tf_op jit(solution)/shard_map/reduce_scatter | solution.py:251
  732.8 921.1 %reduce-scatter.21.cloned.1.call-start = ((), (), s32[]{:S(2)}) async-start(), calls=%async_computation.14 | async-start | bytes 17301504 | tf_op jit(solution)/shard_map/reduce_scatter | solution.py:250
  747.8 8.4 copy-start.16
  747.8 8.7 copy-start.19
  747.8 8.7 copy-start.21
  757.3 47.9 %copy-start.40 = (f32[256]{0:T(256)S(1)}, f32[256]{0:T(256)}, u32[]{:S(2)}) copy-start(f32[256]{0:T(256)} %copy-done.39) | copy-start | bytes 3076
  (67 other events, 214.5 us)
Sparse Core Ops, SparseCore 0:
  13.5 75.8 all-gather.6
  92.2 73.1 all-gather.4
  506.0 103.3 reduce-scatter.10
  613.3 104.5 reduce-scatter.8
  720.6 125.7 reduce-scatter.18
  849.1 137.0 reduce-scatter.12
  989.1 137.4 reduce-scatter.16
  1129.4 137.2 reduce-scatter.14
  1269.7 195.9 reduce-scatter.22
  1468.4 185.3 reduce-scatter.20
where the time goes:
time: 1670 us; the launch traced here: 1660 us
  waiting for transfers between devices  1180 us (71%)
  matrix products  203 us (12%)
  local copies, waits for them, and re-layouts  118 us (7%)
  other arithmetic  85 us (5%)
  blocking collectives  40 us (2%)
  loops' own time  17 us (1%)
    reduce_scatter x1, waiting for transfers between devices, on_device(): lax.psum_scatter(grad_down, ('scene', 'seq'), scatter_dimension=0, tiled=...  199 us
    reduce_scatter x1, waiting for transfers between devices, on_device(): lax.psum_scatter(grad_up, ('scene', 'seq'), scatter_dimension=0, tiled=True)  188 us
    reduce_scatter x1, waiting for transfers between devices, on_device(): lax.psum_scatter(grad_value, ('scene', 'seq'), scatter_dimension=0, tiled...  140 us
    reduce_scatter x1, waiting for transfers between devices, on_device(): lax.psum_scatter(grad_key, ('scene', 'seq'), scatter_dimension=0, tiled=T...  140 us
    reduce_scatter x1, waiting for transfers between devices, on_device(): lax.psum_scatter(grad_query, ('scene', 'seq'), scatter_dimension=0, tiled...  140 us
    reduce_scatter x1, waiting for transfers between devices, on_device(): lax.psum_scatter(k_parts.astype(jnp.bfloat16), 'seq', scatter_dimension=2...  105 us
    reduce_scatter x1, waiting for transfers between devices, on_device(): lax.psum_scatter(v_parts.astype(jnp.bfloat16), 'seq', scatter_dimension=2...  95.1 us
    all_gather x1, waiting for transfers between devices, on_device(): lax.all_gather(k_scene, 'seq', axis=1, tiled=True)  70.9 us
  transfers between devices with their start and end apart: 10, of which 10 were waited for; matrix products, arithmetic and copies ran while one was open for 4% of the time, Pallas kernels for 0%

commit v1 on v0

--- a/solution.py
+++ b/solution.py
@@ -8,6 +8,19 @@
 norm_eps = 1e-05
 score_scale = 0.125
 gelu_coef = 0.7978845608028654
+
+
+def collect(shard, axis, dim):
+    ways = lax.axis_size(axis)
+    up = [(d, (d + 1) % ways) for d in range(ways)]
+    down = [(d, (d - 1) % ways) for d in range(ways)]
+    earlier, later = ([shard], [shard])
+    for _ in range(ways // 2):
+        earlier.append(lax.ppermute(earlier[-1], axis, up))
+    for _ in range((ways - 1) // 2):
+        later.append(lax.ppermute(later[-1], axis, down))
+    line = jnp.concatenate([*earlier[::-1], *later[1:]], axis=dim)
+    return jnp.roll(line, (lax.axis_index(axis) - ways // 2) * shard.shape[dim], axis=dim)
 
 
 def norm_rows(values, gain, shift):
@@ -159,7 +172,7 @@
     k_scene = k_low.reshape(scenes, local_len, model_width)
     v_scene = v_low.reshape(scenes, local_len, model_width)
     k_gathered, v_gathered = (
-        lax.all_gather(k_scene, "seq", axis=1, tiled=True),
+        collect(k_scene, "seq", 1),
         lax.all_gather(v_scene, "seq", axis=1, tiled=True),
     )
     attended, row_lse = attend(q_scene, k_gathered, v_gathered)

time: 1670 us -> 1770 us (1.060)
  matrix products: 203 us -> 258 us
  local copies, waits for them, and re-layouts: 118 us -> 170 us
  waiting for transfers between devices: 1180 us -> 1150 us
  starting transfers between devices: 0.62 us -> 22.5 us
    ppermute x0 -> x15, waiting for transfers between devices: none -> 102 us  [the longest x7 77.4 us: collect(): later.append(lax.ppermute(later[-1], axis, down))]
    reduce_scatter x1, waiting for transfers between devices: 38.4 us -> 140 us  [on_device(): lax.psum_scatter(grad_out, ('scene', 'seq'), scatter_dimension=0, tiled=T...]
    reduce_scatter x1, waiting for transfers between devices: 140 us -> 38.4 us  [on_device(): lax.psum_scatter(grad_query, ('scene', 'seq'), scatter_dimension=0, tiled...]
    all_gather x1 -> x0, waiting for transfers between devices: 70.9 us -> none  [on_device(): lax.all_gather(k_scene, 'seq', axis=1, tiled=True)]
    all_gather x1, waiting for transfers between devices: 64.6 us -> 0.01 us  [on_device(): lax.all_gather(v_scene, 'seq', axis=1, tiled=True)]
    unnamed x107 -> x166, local copies, waits for them, and re-layouts: 10.5 us -> 52.8 us
    dot_general x8, matrix products: 10.2 us -> 36.2 us  [query_pair_step(): jnp.einsum('sqhe,skhe->shqk', d_pair, v_pair, preferred_element_type=jnp....]
    ppermute x0 -> x15, starting transfers between devices: none -> 21.9 us  [the longest x8 15.7 us: collect(): earlier.append(lax.ppermute(earlier[-1], axis, up))]
  transfers between devices with their start and end apart: 10 -> 24, of which waited for: 10 -> 19; matrix products, arithmetic and copies ran while one was open for 4% -> 7% of each run, Pallas kernels for 0% -> 0%
where the time goes in v1:
time: 1770 us; the launch traced here: 1760 us
  waiting for transfers between devices  1150 us (65%)
  matrix products  258 us (15%)
  local copies, waits for them, and re-layouts  170 us (10%)
  other arithmetic  86.4 us (5%)
  blocking collectives  39.7 us (2%)
  starting transfers between devices  22.5 us (1%)
    reduce_scatter x1, waiting for transfers between devices, on_device(): lax.psum_scatter(grad_up, ('scene', 'seq'), scatter_dimension=0, tiled=True)  200 us
    reduce_scatter x1, waiting for transfers between devices, on_device(): lax.psum_scatter(grad_down, ('scene', 'seq'), scatter_dimension=0, tiled=...  188 us
    reduce_scatter x1, waiting for transfers between devices, on_device(): lax.psum_scatter(grad_key, ('scene', 'seq'), scatter_dimension=0, tiled=T...  140 us
    reduce_scatter x1, waiting for transfers between devices, on_device(): lax.psum_scatter(grad_value, ('scene', 'seq'), scatter_dimension=0, tiled...  140 us
    reduce_scatter x1, waiting for transfers between devices, on_device(): lax.psum_scatter(grad_out, ('scene', 'seq'), scatter_dimension=0, tiled=T...  140 us
    reduce_scatter x1, waiting for transfers between devices, on_device(): lax.psum_scatter(v_parts.astype(jnp.bfloat16), 'seq', scatter_dimension=2...  105 us
    reduce_scatter x1, waiting for transfers between devices, on_device(): lax.psum_scatter(k_parts.astype(jnp.bfloat16), 'seq', scatter_dimension=2...  96.4 us
    ppermute x7, waiting for transfers between devices, collect(): later.append(lax.ppermute(later[-1], axis, down))  77.4 us
  transfers between devices with their start and end apart: 24, of which 19 were waited for; matrix products, arithmetic and copies ran while one was open for 7% of the time, Pallas kernels for 0%

profile of v1, /device:TPU:9, one launch (start us, length us, event | category | flops | bytes accessed | tf_op | source)
XLA Modules:
  0.0 1759.1 jit_solution(11596859226097761331)
XLA Ops:
  25.9 9.9 collective-permute-done.1
  50.6 24.0 %collective-permute-done.9 = bf16[1,256,1024]{2,1,0:T(8,128)(2,1)S(1)} collective-permute-done((bf16[1,256,1024]{2,1,0:T(8,128)(2,1)S(1)}, bf16[1,256,1024]{2,1,0:T(8,128)(2,1)S(1)}, u32[]{:S(2)}, u32[]{:S(2)}) %collective-permute-start.9) | collective-permute-done | bytes 524320 | tf_op jit(solution)/shard_map/ppermute | solution.py:21
  76.4 28.7 %collective-permute-done.10 = bf16[1,256,1024]{2,1,0:T(8,128)(2,1)S(1)} collective-permute-done((bf16[1,256,1024]{2,1,0:T(8,128)(2,1)S(1)}, bf16[1,256,1024]{2,1,0:T(8,128)(2,1)S(1)}, u32[]{:S(2)}, u32[]{:S(2)}) %collective-permute-start.10) | collective-permute-done | bytes 524320 | tf_op jit(solution)/shard_map/ppermute | solution.py:21
  106.9 7.9 collective-permute-done.11
  120.3 13.0 collective-permute-done.12
  189.1 7.6 constant_dynamic-slice_fusion.7
  196.6 11.8 copy.44
  208.4 11.7 copy.42
  220.2 71.3 %while.26 = (s32[]{:T(128)}, bf16[8,1,256,128]{2,3,1,0:T(8,128)(2,1)S(1)}, f32[8,1,2,256]{3,2,1,0:T(2,128)S(1)}, s32[8]{0:T(128)S(1)}, bf16[1,4096,1024]{1,2,0:T...) while((s32[]{:T(128)}, ...), condition=%wide.region_5.6_spmd, body=%wide.region_2.5_spmd.sunk | while | flops 555744768 | bytes 31867072 | solution.py:100
  319.8 282.4 %while.27 = (s32[]{:T(128)}, bf16[8,1,256,128]{2,3,1,0:T(8,128)(2,1)}, bf16[8,1,4096,128]{2,3,1,0:T(8,128)(2,1)}, bf16[8,1,4096,128]{2,3,1,0:T(8,128)(2,1)}, s32...) while((s32[]{:T(128)}, ...), condition=%wide.region_12.13_spmd, body=%wide.region_10.12_spmd.sunk | while | flops 1360068096 | bytes 81602872 | solution.py:137
  337.4 7.9 multiply_convert_fusion.5
  372.7 7.9 multiply_convert_fusion.5
  408.0 7.9 multiply_convert_fusion.5
  436.7 6.6 multiply_reduce_fusion.8
  443.3 7.9 multiply_convert_fusion.5
  478.5 7.9 multiply_convert_fusion.5
  513.9 7.9 multiply_convert_fusion.5
  549.2 7.9 multiply_convert_fusion.5
  577.8 6.6 multiply_reduce_fusion.8
  584.4 7.9 multiply_convert_fusion.5
  610.7 96.4 %reduce-scatter.9.cloned.1.call-done = bf16[8,1,256,128]{2,3,1,0:T(8,128)(2,1)} async-done(((bf16[8,1,4096,128]{2,3,1,0:T(8,128)(2,1)}), bf16[8,1,256,128]{2,3,1,0:T(8,128)(2,1)}) %reduce-scatter.9.cloned.1.call-update) | async-done | bytes 524304 | tf_op jit(solution)/shard_map/reduce_scatter | solution.py:210
  711.0 104.7 %reduce-scatter.11.cloned.1.call-done = bf16[8,1,256,128]{2,3,1,0:T(8,128)(2,1)} async-done(((bf16[8,1,4096,128]{2,3,1,0:T(8,128)(2,1)}), bf16[8,1,256,128]{2,3,1,0:T(8,128)(2,1)}) %reduce-scatter.11.cloned.1.call-update) | async-done | bytes 524304 | tf_op jit(solution)/shard_map/reduce_scatter | solution.py:213
  819.7 10.2 fusion.45
  831.0 10.9 fusion.40
  845.9 8.6 fusion.24
  858.1 39.7 %all-reduce.9 = (f32[1024]{0:T(1024)S(1)}, f32[1024]{0:T(1024)S(1)}, f32[1024]{0:T(1024)S(1)}, f32[4096]{0:T(1024)S(1)}, f32[1024]{0:T(1024)S(1)}, /*index=5*/f3...) all-reduce(f32[1024]{0:T(1024)S(1)} %bitcast.240, ...), channel_id=11, replica_groups=mesh['scene'=2,'seq'=16] {'scene','seq'}, use_global_device_ids=true, to_apply=%region_24.25.clone | all-reduce | flops 12288 | bytes 98304
  905.9 38.4 %reduce-scatter.13.cloned.1.call-done = f32[32,1024]{1,0:T(8,128)} async-done(((f32[1024,1024]{1,0:T(8,128)}), f32[32,1024]{1,0:T(8,128)}) %reduce-scatter.13.cloned.1.call-update) | async-done | bytes 131088 | tf_op jit(solution)/shard_map/reduce_scatter | solution.py:254
  944.2 140.0 %reduce-scatter.19.cloned.1.call-done = f32[32,1024]{1,0:T(8,128)} async-done(((f32[1024,1024]{1,0:T(8,128)}), f32[32,1024]{1,0:T(8,128)}) %reduce-scatter.19.cloned.1.call-update) | async-done | bytes 131088 | tf_op jit(solution)/shard_map/reduce_scatter | solution.py:257
  1084.2 140.4 %reduce-scatter.15.cloned.1.call-done = f32[32,1024]{1,0:T(8,128)} async-done(((f32[1024,1024]{1,0:T(8,128)}), f32[32,1024]{1,0:T(8,128)}) %reduce-scatter.15.cloned.1.call-update) | async-done | bytes 131088 | tf_op jit(solution)/shard_map/reduce_scatter | solution.py:255
  1224.7 140.2 %reduce-scatter.17.cloned.1.call-done = f32[32,1024]{1,0:T(8,128)} async-done(((f32[1024,1024]{1,0:T(8,128)}), f32[32,1024]{1,0:T(8,128)}) %reduce-scatter.17.cloned.1.call-update) | async-done | bytes 131088 | tf_op jit(solution)/shard_map/reduce_scatter | solution.py:256
  1364.8 199.7 %reduce-scatter.21.cloned.1.call-done = f32[32,4096]{1,0:T(8,128)} async-done(((f32[1024,4096]{1,0:T(8,128)}), f32[32,4096]{1,0:T(8,128)}) %reduce-scatter.21.cloned.1.call-update) | async-done | bytes 524304 | tf_op jit(solution)/shard_map/reduce_scatter | solution.py:263
  1564.5 187.9 %reduce-scatter.23.cloned.1.call-done = f32[128,1024]{1,0:T(8,128)} async-done(((f32[4096,1024]{1,0:T(8,128)}), f32[128,1024]{1,0:T(8,128)}) %reduce-scatter.23.cloned.1.call-update) | async-done | bytes 524304 | tf_op jit(solution)/shard_map/reduce_scatter | solution.py:264
  (446 shorter events, 419.6 us)
Async XLA Ops:
  7.2 128.0 %copy-start.2 = (bf16[1,256,1024]{2,1,0:T(8,128)(2,1)S(1)}, bf16[1,256,1024]{2,1,0:T(8,128)(2,1)}, u32[]{:S(2)}) copy-start(bf16[1,256,1024]{2,1,0:T(8,128)(2,1)} %param.22) | copy-start | bytes 1572868
  7.2 128.0 %copy-start.43 = (f32[1024]{0:T(1024)S(1)}, f32[1024]{0:T(1024)}, u32[]{:S(2)}) copy-start(f32[1024]{0:T(1024)} %param.37) | copy-start | bytes 12292
  7.2 128.0 %copy-start.38 = (f32[1024]{0:T(1024)S(1)}, f32[1024]{0:T(1024)}, u32[]{:S(2)}) copy-start(f32[1024]{0:T(1024)} %param.36) | copy-start | bytes 12292
  7.2 128.0 %copy-start.58 = (f32[1024]{0:T(1024)S(1)}, f32[1024]{0:T(1024)}, u32[]{:S(2)}) copy-start(f32[1024]{0:T(1024)} %param.31) | copy-start | bytes 12292
  7.2 201.2 %all-gather.3.cloned.1.call-start = ((), (), s32[]{:S(2)}) async-start(), calls=%async_computation.16 | async-start | bytes 8912896 | tf_op jit(solution)/shard_map/all_gather | solution.py:176
  8.6 131.8 %copy-start.56 = (s32[1,256]{1,0:T(1,128)S(1)}, s32[1,256]{1,0:T(1,128)}, u32[]{:S(2)}) copy-start(s32[1,256]{1,0:T(1,128)} %param.23) | copy-start | bytes 3076
  8.7 140.5 %copy-start.41 = (f32[256]{0:T(256)}, f32[256]{0:T(256)S(1)}, u32[]{:S(2)}) copy-start(f32[256]{0:T(256)S(1)} %broadcast_multiply_fusion.1) | copy-start | bytes 3076
  10.0 139.1 %copy-start.45 = (f32[256]{0:T(256)}, f32[256]{0:T(256)S(1)}, u32[]{:S(2)}) copy-start(f32[256]{0:T(256)S(1)} %fusion.42) | copy-start | bytes 3076
  12.7 694.4 %reduce-scatter.9.cloned.1.call-start = ((), (), s32[]{:S(2)}) async-start(), calls=%async_computation.8 | async-start | bytes 8912896 | tf_op jit(solution)/shard_map/reduce_scatter | solution.py:210
  15.3 8.0 collective-permute-start
  23.3 12.5 collective-permute-start.1
  25.8 14.3 collective-permute-start.8
  35.7 12.3 collective-permute-start.2
  40.2 34.4 %collective-permute-start.9 = (bf16[1,256,1024]{2,1,0:T(8,128)(2,1)S(1)}, bf16[1,256,1024]{2,1,0:T(8,128)(2,1)S(1)}, u32[]{:S(2)}, u32[]{:S(2)}) collective-permute-start(bf16[1,256,1024]{2,1,0:T(8,128)(2,1)S(1)} %collective-permute-done.8), channel_id=1, source_target_pairs={{0,15},{1,0},{2,1},{3,2},{4,3},{5,4},{6,5},{7,6},{8,7},{9,8},{10,9... | collective-permute-start | bytes 1572872 | tf_op jit(solution)/shard_map/ppermute | solution.py:21
  48.1 27.3 %collective-permute-start.3 = (bf16[1,256,1024]{2,1,0:T(8,128)(2,1)S(1)}, bf16[1,256,1024]{2,1,0:T(8,128)(2,1)S(1)}, u32[]{:S(2)}, u32[]{:S(2)}) collective-permute-start(bf16[1,256,1024]{2,1,0:T(8,128)(2,1)S(1)} %collective-permute-done.2), channel_id=1, source_target_pairs={{0,1},{1,2},{2,3},{3,4},{4,5},{5,6},{6,7},{7,8},{8,9},{9,10},{10,1... | collective-permute-start | bytes 1572872 | tf_op jit(solution)/shard_map/ppermute | solution.py:19
  74.6 30.5 %collective-permute-start.10 = (bf16[1,256,1024]{2,1,0:T(8,128)(2,1)S(1)}, bf16[1,256,1024]{2,1,0:T(8,128)(2,1)S(1)}, u32[]{:S(2)}, u32[]{:S(2)}) collective-permute-start(bf16[1,256,1024]{2,1,0:T(8,128)(2,1)S(1)} %collective-permute-done.9), channel_id=1, source_target_pairs={{0,15},{1,0},{2,1},{3,2},{4,3},{5,4},{6,5},{7,6},{8,7},{9,8},{10,9... | collective-permute-start | bytes 1572872 | tf_op jit(solution)/shard_map/ppermute | solution.py:21
  75.4 30.5 %collective-permute-start.4 = (bf16[1,256,1024]{2,1,0:T(8,128)(2,1)S(1)}, bf16[1,256,1024]{2,1,0:T(8,128)(2,1)S(1)}, u32[]{:S(2)}, u32[]{:S(2)}) collective-permute-start(bf16[1,256,1024]{2,1,0:T(8,128)(2,1)S(1)} %collective-permute-done.3), channel_id=1, source_target_pairs={{0,1},{1,2},{2,3},{3,4},{4,5},{5,6},{6,7},{7,8},{8,9},{9,10},{10,1... | collective-permute-start | bytes 1572872 | tf_op jit(solution)/shard_map/ppermute | solution.py:19
  105.1 9.7 collective-permute-start.11
  105.9 11.9 collective-permute-start.5
  115.6 17.7 %collective-permute-start.12 = (bf16[1,256,1024]{2,1,0:T(8,128)(2,1)S(1)}, bf16[1,256,1024]{2,1,0:T(8,128)(2,1)}, u32[]{:S(2)}, u32[]{:S(2)}) collective-permute-start(bf16[1,256,1024]{2,1,0:T(8,128)(2,1)S(1)} %collective-permute-done.11), channel_id=1, source_target_pairs={{0,15},{1,0},{2,1},{3,2},{4,3},{5,4},{6,5},{7,6},{8,7},{9,8},{10,9... | collective-permute-start | bytes 1572872 | tf_op jit(solution)/shard_map/ppermute | solution.py:21
  117.8 15.6 collective-permute-start.6
  133.4 8.9 collective-permute-start.13
  133.4 13.9 collective-permute-start.7
  142.3 28.4 %collective-permute-start.14 = (bf16[1,256,1024]{2,1,0:T(8,128)(2,1)}, bf16[1,256,1024]{2,1,0:T(8,128)(2,1)S(1)}, u32[]{:S(2)}, u32[]{:S(2)}) collective-permute-start(bf16[1,256,1024]{2,1,0:T(8,128)(2,1)} %collective-permute-done.13), channel_id=1, source_target_pairs={{0,15},{1,0},{2,1},{3,2},{4,3},{5,4},{6,5},{7,6},{8,7},{9,8},{10,9... | collective-permute-start | bytes 1572872 | tf_op jit(solution)/shard_map/ppermute | solution.py:21
  220.2 74.3 %copy-start.37 = (f32[1024]{0:T(1024)S(1)}, f32[1024]{0:T(1024)}, u32[]{:S(2)}) copy-start(f32[1024]{0:T(1024)} %param.38) | copy-start | bytes 12292
  602.3 213.5 %reduce-scatter.11.cloned.1.call-start = ((), (), s32[]{:S(2)}) async-start(), calls=%async_computation.9 | async-start | bytes 8912896 | tf_op jit(solution)/shard_map/reduce_scatter | solution.py:213
  603.0 341.2 %reduce-scatter.13.cloned.1.call-start = ((), (), s32[]{:S(2)}) async-start(), calls=%async_computation.10 | async-start | bytes 4325376 | tf_op jit(solution)/shard_map/reduce_scatter | solution.py:254
  606.4 477.8 %reduce-scatter.19.cloned.1.call-start = ((), (), s32[]{:S(2)}) async-start(), calls=%async_computation.13 | async-start | bytes 4325376 | tf_op jit(solution)/shard_map/reduce_scatter | solution.py:257
  610.6 614.0 %reduce-scatter.15.cloned.1.call-start = ((), (), s32[]{:S(2)}) async-start(), calls=%async_computation.11 | async-start | bytes 4325376 | tf_op jit(solution)/shard_map/reduce_scatter | solution.py:255
  711.0 653.8 %reduce-scatter.17.cloned.1.call-start = ((), (), s32[]{:S(2)}) async-start(), calls=%async_computation.12 | async-start | bytes 4325376 | tf_op jit(solution)/shard_map/reduce_scatter | solution.py:256
  819.7 744.8 %reduce-scatter.21.cloned.1.call-start = ((), (), s32[]{:S(2)}) async-start(), calls=%async_computation.14 | async-start | bytes 17301504 | tf_op jit(solution)/shard_map/reduce_scatter | solution.py:263
  830.0 922.4 %reduce-scatter.23.cloned.1.call-start = ((), (), s32[]{:S(2)}) async-start(), calls=%async_computation.15 | async-start | bytes 17301504 | tf_op jit(solution)/shard_map/reduce_scatter | solution.py:264
  (63 other events, 975.2 us)
Sparse Core Ops, SparseCore 0:
  12.8 115.3 all-gather.2
  602.4 104.6 reduce-scatter.8
  711.1 104.5 reduce-scatter.10
  818.5 125.7 reduce-scatter.12
  946.9 137.2 reduce-scatter.18
  1086.9 137.6 reduce-scatter.14
  1227.5 137.2 reduce-scatter.16
  1367.7 196.7 reduce-scatter.20
  1567.4 184.9 reduce-scatter.22
